TPU v7x, 256 devices: a whole 4x4x8 slice. The times are simulated.
256 devices in a mesh: ctx: 32 (over y, z_lo, core), tp: 8 (over x, z_hi).
Axes of the slice: x: 4, y: 4, z: 8 (z_hi: 2, z_lo: 4; z = z_hi * 4 + z_lo), core: 2. Of those that a mesh axis runs over, the one named last changes fastest.
Arguments:
- tokens: bfloat16 [12288, 3072], P('ctx', 'tp'), may hold values from -6 to 6
- queries: bfloat16 [12288, 2048], P('ctx', 'tp'), may hold values from -16 to 16
- key_rows: bfloat16 [12288, 2048], P('ctx', 'tp'), may hold values from -16 to 16
- value_rows: bfloat16 [12288, 2048], P('ctx', 'tp'), may hold values from -6 to 6
- clip_ids: int32 [12288], replicated, may hold values from 0 to 3, never falling along the last dimension, each value on 1 to 9216 neighbouring positions
- causal: int32 [4], replicated, may hold values 0 or 1
- modulation: float32 [3, 4, 3072], replicated, may hold values from -3 to 3
- w_mlp: bfloat16 [3072, 6144], P(None, 'tp'), may hold values from -0.109375 to 0.109375
- w_attn_out: bfloat16 [2048, 3072], P('tp'), may hold values from -1 to 1
- w_mlp_out: bfloat16 [6144, 3072], P('tp'), may hold values from -0.078125 to 0.078125
Outputs:
- mixed: float32 [12288, 3072], P(('ctx', 'tp'))
Inputs may be any that keep to these rules, and one draw needn't show every extreme that they name: `clip_ids`: clip numbers never fall along the tokens; each of the 4 clips has 1 to 9216 tokens and one has exactly 9216.
All inputs are finite; a program needn't handle non-finite values.
Results may differ from a plain program's by a relative error of at most 0.0065.
Values may be sent and summed in bfloat16 or wider, within the bound.
A program may use at most 128 MiB of HBM per device.

v0:
```python
import math
import jax
import jax.numpy as jnp
from jax import lax
from jax.sharding import PartitionSpec as P

HD = 128
neg_large = -1e30
eps_norm = 1e-06


def per_token(clip_rows, table):
    onehot = (clip_rows[:, None] == jnp.arange(table.shape[0], dtype=jnp.int32)[None, :]).astype(
        jnp.float32
    )
    return jnp.dot(onehot, table, precision=lax.Precision.HIGHEST)


def causal_rows(clip_rows, causal):
    matches = clip_rows[:, None] == jnp.arange(causal.shape[0], dtype=jnp.int32)[None, :]
    return jnp.sum(jnp.where(matches, causal[None, :], 0), axis=1)


def visible(query_ids, query_pos, query_causal, key_ids, key_pos):
    same_clip = query_ids[:, None] == key_ids[None, :]
    earlier = key_pos[None, :] <= query_pos[:, None]
    return same_clip & ((query_causal[:, None] == 0) | earlier)


def attend(carry_state, query_tile, allowed, key_tile, value_tile, inverse_root):
    numerator, running_max, denominator = carry_state
    scores = (
        jnp.einsum("ihd,jhd->hij", query_tile, key_tile, preferred_element_type=jnp.float32)
        * inverse_root
    )
    scores = jnp.where(allowed[None], scores, neg_large)
    new_max = jnp.maximum(running_max, jnp.transpose(jnp.max(scores, axis=2)))
    weights = jnp.where(allowed[None], jnp.exp(scores - jnp.transpose(new_max)[:, :, None]), 0.0)
    rounded = weights.astype(jnp.bfloat16)
    factor = jnp.exp(running_max - new_max)
    numerator = numerator * factor[:, :, None] + jnp.einsum(
        "hij,jhd->ihd", rounded, value_tile, preferred_element_type=jnp.float32
    )
    denominator = denominator * factor + jnp.transpose(jnp.sum(rounded.astype(jnp.float32), axis=2))
    return (numerator, new_max, denominator)


def attend_some(carry_state, query_tile, allowed, key_tile, value_tile, inverse_root):
    return attend(carry_state, query_tile, allowed, key_tile, value_tile, inverse_root)


def per_device(
    tokens,
    queries,
    key_rows,
    value_rows,
    clip_ids,
    causal,
    modulation,
    w_mlp,
    w_attn_out,
    w_mlp_out,
):
    local_rows = queries.shape[0]
    heads_local = queries.shape[1] // HD
    inverse_root = 1.0 / math.sqrt(HD)
    tp_size = lax.axis_size("tp")
    first_row = lax.axis_index("ctx") * local_rows
    own_pos = first_row + jnp.arange(local_rows, dtype=jnp.int32)
    own_ids = lax.dynamic_slice_in_dim(clip_ids, first_row, local_rows)
    own_causal = causal_rows(own_ids, causal)
    own_query = queries.reshape(local_rows, heads_local, HD)
    start_state = (
        jnp.zeros((local_rows, heads_local, HD), jnp.float32),
        jnp.full((local_rows, heads_local), neg_large, jnp.float32),
        jnp.zeros((local_rows, heads_local), jnp.float32),
    )
    whole_rows = lax.all_gather(tokens, "tp", axis=1, tiled=True)
    token_values = whole_rows.astype(jnp.float32)
    row_mean = jnp.mean(token_values, axis=1, keepdims=True)
    centred = token_values - row_mean
    row_var = jnp.mean(centred * centred, axis=1, keepdims=True)
    normed = centred * lax.rsqrt(row_var + eps_norm)
    shift_rows = per_token(own_ids, modulation[0])
    scale_rows = per_token(own_ids, modulation[1])
    modulated = (normed * (1.0 + scale_rows) + shift_rows).astype(jnp.bfloat16)
    hidden = jax.nn.gelu(
        jnp.dot(modulated, w_mlp, preferred_element_type=jnp.float32), approximate=True
    ).astype(jnp.bfloat16)
    carry_state = start_state
    key_piece = lax.all_gather(key_rows, "ctx", axis=0, tiled=True)
    value_piece = lax.all_gather(value_rows, "ctx", axis=0, tiled=True)
    piece_rows = key_piece.shape[0]
    tile_rows = piece_rows
    tile_rows = local_rows * math.gcd(piece_rows // local_rows, 4)

    def one_tile(inner_state, tile_index):
        offset = tile_index * tile_rows
        key_tile = lax.dynamic_slice_in_dim(key_piece, offset, tile_rows, 0).reshape(
            tile_rows, heads_local, HD
        )
        value_tile = lax.dynamic_slice_in_dim(value_piece, offset, tile_rows, 0).reshape(
            tile_rows, heads_local, HD
        )
        key_pos = offset + jnp.arange(tile_rows, dtype=jnp.int32)
        key_ids = lax.dynamic_slice_in_dim(clip_ids, offset, tile_rows)
        allowed = visible(own_ids, own_pos, own_causal, key_ids, key_pos)
        return (
            attend_some(inner_state, own_query, allowed, key_tile, value_tile, inverse_root),
            None,
        )

    carry_state, _ = lax.scan(
        one_tile, carry_state, jnp.arange(piece_rows // tile_rows, dtype=jnp.int32)
    )
    numerator, running_max, denominator = carry_state
    attended = (
        (numerator / denominator[:, :, None])
        .astype(jnp.bfloat16)
        .reshape(local_rows, heads_local * HD)
    )
    share_rows = local_rows // tp_size
    branch = lax.psum_scatter(
        jnp.dot(attended, w_attn_out, preferred_element_type=jnp.float32)
        + jnp.dot(hidden, w_mlp_out, preferred_element_type=jnp.float32),
        "tp",
        scatter_dimension=0,
        tiled=True,
    )
    first_share = lax.axis_index("tp") * share_rows
    residual = lax.dynamic_slice_in_dim(token_values, first_share, share_rows, 0)
    gate_rows = lax.dynamic_slice_in_dim(
        per_token(own_ids, modulation[2]), first_share, share_rows, 0
    )
    return residual + gate_rows * branch


def solution(mesh):
    in_specs = (
        P("ctx", "tp"),
        P("ctx", "tp"),
        P("ctx", "tp"),
        P("ctx", "tp"),
        P(),
        P(),
        P(),
        P(None, "tp"),
        P("tp", None),
        P("tp", None),
    )
    out_specs = P(("ctx", "tp"), None)
    return jax.shard_map(
        per_device, mesh=mesh, in_specs=in_specs, out_specs=out_specs, check_vma=False
    )
```

profile of v0, /device:TPU:1, one launch (start us, length us, event | category | flops | bytes accessed | tf_op | source)
XLA Modules:
  0.0 494.2 jit_solution(2514441145359709445)
XLA Ops:
  7.3 1.7 copy.21
  9.1 1.8 copy.23
  14.3 4.9 %fusion.19 = f32[384,3072]{1,0:T(8,128)} fusion(f32[3,4,3072]{2,1,0:T(4,128)} %param.18, s32[384]{0:T(512)S(1)} %dynamic_slice.23), kind=kOutput, calls=%fused_computation.40 | convolution fusion | flops 56624640 | bytes 4769280 | tf_op jit(solution)/shard_map/dot_general | solution.py:16
  19.3 74.0 %all-gather.4.cloned.1.call-done = bf16[384,3072]{1,0:T(8,128)(2,1)} async-done(((bf16[384,384]{1,0:T(8,128)(2,1)}), bf16[384,3072]{1,0:T(8,128)(2,1)}) %all-gather.4.cloned.1.call-update) | async-done | bytes 2359312 | tf_op jit(solution)/shard_map/all_gather | solution.py:78
  93.3 2.2 convert_reduce_fusion.1
  95.5 2.4 multiply_reduce_fusion
  98.0 6.9 %add_convert_fusion = bf16[384,3072]{1,0:T(8,128)(2,1)} fusion(f32[384,3072]{1,0:T(8,128)} %fusion.19, bf16[384,3072]{1,0:T(8,128)(2,1)S(1)} %copy-done.2, f32[384]{0:T(512)S(1)} %add_rsqrt_fusion, f32[384]{0:T(512)S(1)} %broadcast_multiply_fusion, f32[3,4,3072]{2,1,0:T(4,128)} %param.18, s32[384]{0:T(512)S(1)} %dynamic_slice.23), kind=kOutput, calls=%fused_computation.19 | convolution fusion | flops 64882176 | bytes 9490944 | tf_op jit(solution)/shard_map/dot_general | solution.py:16
  104.9 11.6 %fusion.12 = f32[384,3072]{1,0:T(8,128)} fusion(bf16[768,3072]{1,0:T(8,128)(2,1)} %param.21, bf16[384,3072]{1,0:T(8,128)(2,1)} %add_convert_fusion, bf16[3072,768]{1,0:T(8,128)(2,1)} %param.19), kind=kOutput, calls=%fused_computation.32 | convolution fusion | flops 3626532864 | bytes 16515072 | tf_op jit(solution)/shard_map/dot_general | solution.py:125
  116.5 42.9 %all-gather.6.cloned.1.call-done = bf16[12288,256]{0,1:T(8,128)(2,1)} async-done(((bf16[384,256]{0,1:T(8,128)(2,1)}), bf16[12288,256]{0,1:T(8,128)(2,1)}) %all-gather.6.cloned.1.call-update) | async-done | bytes 6291472 | tf_op jit(solution)/shard_map/all_gather | solution.py:91
  159.4 68.4 %all-gather.8.cloned.1.call-done = bf16[12288,256]{0,1:T(8,128)(2,1)} async-done(((bf16[384,256]{0,1:T(8,128)(2,1)}), bf16[12288,256]{0,1:T(8,128)(2,1)}) %all-gather.8.cloned.1.call-update) | async-done | bytes 6291472 | tf_op jit(solution)/shard_map/all_gather | solution.py:92
  228.3 118.4 %while.15 = (s32[]{:T(128)}, f32[384,2,128]{0,2,1:T(8,128)S(1)}, f32[384,2]{0,1:T(2,128)S(1)}, f32[384,2]{0,1:T(2,128)S(1)}, s32[384]{0:T(512)S(1)}, /*index=5*/...) while((s32[]{:T(128)}, f32[384,2,128]{0,2,1:T(8,128)S(1)}, ...), condition=%wide.region_4.5_spmd.clone, body=%wide.region_1.4_spmd.clone.sunk | while | flops 624334848 | bytes 41178116 | solution.py:113
  234.3 3.3 fusion.51
  237.6 3.7 convert_reduce_fusion.3
  249.1 3.3 fusion.51
  252.4 3.7 convert_reduce_fusion.3
  263.9 3.3 fusion.51
  267.2 3.7 convert_reduce_fusion.3
  278.7 3.3 fusion.51
  282.0 3.7 convert_reduce_fusion.3
  293.5 3.3 fusion.51
  296.8 3.7 convert_reduce_fusion.3
  308.3 3.3 fusion.51
  311.6 3.7 convert_reduce_fusion.3
  323.1 3.3 fusion.51
  326.4 3.7 convert_reduce_fusion.3
  337.9 3.3 fusion.51
  341.2 3.7 convert_reduce_fusion.3
  346.7 5.3 %convolution_add_fusion = f32[384,3072]{1,0:T(8,128)} fusion(f32[384,3072]{1,0:T(8,128)} %fusion.12, bf16[384,256]{0,1:T(8,128)(2,1)S(1)} %bitcast.71, bf16[256,3072]{1,0:T(8,128)(2,1)S(1)} %copy-done), kind=kOutput, calls=%fused_computation.21 | convolution fusion | flops 605159424 | bytes 11206656 | tf_op jit(solution)/shard_map/dot_general | solution.py:124
  352.0 5.1 %fusion.21 = f32[384,3072]{1,0:T(8,128)} fusion(f32[3,4,3072]{2,1,0:T(4,128)} %param.18, s32[384]{0:T(512)S(1)} %get-tuple-element.315), kind=kOutput, calls=%fused_computation.42 | convolution fusion | flops 56624640 | bytes 4769280 | tf_op jit(solution)/shard_map/dot_general | solution.py:16
  357.1 2.7 convert_element_type.21
  359.9 125.5 %reduce-scatter.2.cloned.1.call-done = f32[48,3072]{1,0:T(8,128)} async-done(((f32[384,3072]{1,0:T(8,128)}), f32[48,3072]{1,0:T(8,128)}) %reduce-scatter.2.cloned.1.call-update) | async-done | bytes 589840 | tf_op jit(solution)/shard_map/reduce_scatter | solution.py:123
  485.4 2.3 multiply_add_fusion
  (129 shorter events, 61.2 us)
Async XLA Ops:
  6.5 340.2 %copy-start = (bf16[256,3072]{1,0:T(8,128)(2,1)S(1)}, bf16[256,3072]{1,0:T(8,128)(2,1)}, u32[]{:S(2)}) copy-start(bf16[256,3072]{1,0:T(8,128)(2,1)} %param.20) | copy-start | bytes 4718596
  6.5 86.8 %all-gather.4.cloned.1.call-start = ((), (), s32[]{:S(2)}) async-start(), calls=%async_computation.1 | async-start | bytes 2654208 | tf_op jit(solution)/shard_map/all_gather | solution.py:78
  7.3 152.1 %all-gather.6.cloned.1.call-start = ((), (), s32[]{:S(2)}) async-start(), calls=%async_computation.2 | async-start | bytes 6488064 | tf_op jit(solution)/shard_map/all_gather | solution.py:91
  9.1 218.7 %all-gather.8.cloned.1.call-start = ((), (), s32[]{:S(2)}) async-start(), calls=%async_computation.3 | async-start | bytes 6488064 | tf_op jit(solution)/shard_map/all_gather | solution.py:92
  10.9 474.5 %reduce-scatter.2.cloned.1.call-start = ((), (), s32[]{:S(2)}) async-start(), calls=%async_computation.4 | async-start | bytes 5308416 | tf_op jit(solution)/shard_map/reduce_scatter | solution.py:123
  93.3 4.6 copy-start.2
  237.6 3.8 copy-start.1
  252.4 3.8 copy-start.1
  267.2 3.8 copy-start.1
  282.0 3.8 copy-start.1
  296.8 3.8 copy-start.1
  311.6 3.8 copy-start.1
  326.4 3.8 copy-start.1
  341.2 3.8 copy-start.1
  352.0 5.1 %copy-start.3 = (bf16[384,3072]{1,0:T(8,128)(2,1)S(1)}, bf16[384,3072]{1,0:T(8,128)(2,1)}, u32[]{:S(2)}) copy-start(bf16[384,3072]{1,0:T(8,128)(2,1)} %all-gather.4.cloned.1.call-done) | copy-start | bytes 7077892
Sparse Core Ops, SparseCore 0:
  9.8 83.4 all-gather.3
  95.1 64.1 all-gather.5
  161.2 66.5 all-gather.7
  352.1 133.2 reduce-scatter.1
where the time goes:
time: 496 us; the launch traced here: 494 us
  waiting for transfers between devices  312 us (63%)
  matrix products  73.8 us (15%)
  other arithmetic  55.2 us (11%)
  local copies, waits for them, and re-layouts  34.7 us (7%)
  between operations  13.2 us (3%)
  loops' own time  5.58 us (1%)
    reduce_scatter x1, waiting for transfers between devices, per_device(): lax.psum_scatter(jnp.dot(attended, w_attn_out, preferred_element_type=jnp...  126 us
    all_gather x1, waiting for transfers between devices, per_device(): whole_rows = lax.all_gather(tokens, 'tp', axis=1, tiled=True)  74 us
    all_gather x1, waiting for transfers between devices, per_device(): value_piece = lax.all_gather(value_rows, 'ctx', axis=0, tiled=True)  68.4 us
    all_gather x1, waiting for transfers between devices, per_device(): key_piece = lax.all_gather(key_rows, 'ctx', axis=0, tiled=True)  42.9 us
    reduce_sum x8, other arithmetic, attend(): jnp.sum(rounded.astype(jnp.float32), axis=2)  29.8 us
    dot_general x8, matrix products, attend(): jnp.einsum('ihd,jhd->hij', query_tile, key_tile, preferred_element_type=j...  26.6 us
    dot_general x3, matrix products, per_token(): return jnp.dot(onehot, table, precision=lax.Precision.HIGHEST)  17 us
    dot_general x8, matrix products, attend(): jnp.einsum('hij,jhd->ihd', rounded, value_tile, preferred_element_type=jn...  13.4 us
  transfers between devices with their start and end apart: 4, of which 4 were waited for; matrix products, arithmetic and copies ran while one was open for 9% of the time, Pallas kernels for 0%

commit v1 on v0

--- a/solution.py
+++ b/solution.py
@@ -88,7 +88,8 @@
         jnp.dot(modulated, w_mlp, preferred_element_type=jnp.float32), approximate=True
     ).astype(jnp.bfloat16)
     carry_state = start_state
-    key_piece = lax.all_gather(key_rows, "ctx", axis=0, tiled=True)
+    sent = jnp.stack([key_rows] * lax.axis_size("ctx"))
+    key_piece = jnp.concatenate(lax.all_to_all(sent, "ctx", 0, 0), axis=0)
     value_piece = lax.all_gather(value_rows, "ctx", axis=0, tiled=True)
     piece_rows = key_piece.shape[0]
     tile_rows = piece_rows

time: 496 us -> 526 us (1.060)
  local copies, waits for them, and re-layouts: 34.7 us -> 69.7 us
  waiting for transfers between devices: 312 us -> 298 us
  starting transfers between devices: 0.13 us -> 10.5 us
    all_to_all x0 -> x1, waiting for transfers between devices: none -> 89.9 us  [per_device(): key_piece = jnp.concatenate(lax.all_to_all(sent, 'ctx', 0, 0), axis=0)]
    all_gather x1, waiting for transfers between devices: 68.4 us -> 0.01 us  [per_device(): value_piece = lax.all_gather(value_rows, 'ctx', axis=0, tiled=True)]
    all_gather x1 -> x0, waiting for transfers between devices: 42.9 us -> none  [per_device(): key_piece = lax.all_gather(key_rows, 'ctx', axis=0, tiled=True)]
    dynamic_slice x0 -> x16, local copies, waits for them, and re-layouts: none -> 28.1 us  [one_tile(): lax.dynamic_slice_in_dim(key_piece, offset, tile_rows, 0)]
    all_to_all x0 -> x1, starting transfers between devices: none -> 10.4 us  [per_device(): key_piece = jnp.concatenate(lax.all_to_all(sent, 'ctx', 0, 0), axis=0)]
    all_to_all x0 -> x1, local copies, waits for them, and re-layouts: none -> 8.61 us  [per_device(): key_piece = jnp.concatenate(lax.all_to_all(sent, 'ctx', 0, 0), axis=0)]
    all_gather x1, waiting for transfers between devices: 74 us -> 82.4 us  [per_device(): whole_rows = lax.all_gather(tokens, 'tp', axis=1, tiled=True)]
  transfers between devices with their start and end apart: 4 -> 4, of which waited for: 4 -> 3; matrix products, arithmetic and copies ran while one was open for 9% -> 10% of each run, Pallas kernels for 0% -> 0%
where the time goes in v1:
time: 526 us; the launch traced here: 523 us
  waiting for transfers between devices  298 us (57%)
  matrix products  72.6 us (14%)
  local copies, waits for them, and re-layouts  69.7 us (13%)
  other arithmetic  54.2 us (10%)
  between operations  13.2 us (3%)
  starting transfers between devices  10.5 us (2%)
    reduce_scatter x1, waiting for transfers between devices, per_device(): lax.psum_scatter(jnp.dot(attended, w_attn_out, preferred_element_type=jnp...  125 us
    all_to_all x1, waiting for transfers between devices, per_device(): key_piece = jnp.concatenate(lax.all_to_all(sent, 'ctx', 0, 0), axis=0)  89.9 us
    all_gather x1, waiting for transfers between devices, per_device(): whole_rows = lax.all_gather(tokens, 'tp', axis=1, tiled=True)  82.4 us
    reduce_sum x8, other arithmetic, attend(): jnp.sum(rounded.astype(jnp.float32), axis=2)  29.8 us
    dynamic_slice x16, local copies, waits for them, and re-layouts, one_tile(): lax.dynamic_slice_in_dim(key_piece, offset, tile_rows, 0)  28.1 us
    dot_general x8, matrix products, attend(): jnp.einsum('ihd,jhd->hij', query_tile, key_tile, preferred_element_type=j...  26.1 us
    dot_general x3, matrix products, per_token(): return jnp.dot(onehot, table, precision=lax.Precision.HIGHEST)  16.2 us
    dot_general x8, matrix products, attend(): jnp.einsum('hij,jhd->ihd', rounded, value_tile, preferred_element_type=jn...  13.4 us
  transfers between devices with their start and end apart: 4, of which 3 were waited for; matrix products, arithmetic and copies ran while one was open for 10% of the time, Pallas kernels for 0%

profile of v1, /device:TPU:1, one launch (start us, length us, event | category | flops | bytes accessed | tf_op | source)
XLA Modules:
  0.0 523.5 jit_solution(7752779272402966335)
XLA Ops:
  8.4 3.6 stack.2
  12.0 10.4 %all-to-all-start = ((bf16[32,384,256]{1,2,0:T(8,128)(2,1)}), bf16[32,384,256]{1,2,0:T(8,128)(2,1)}, u32[]{:S(2)}, u32[]{:S(2)}) async-start(bf16[32,384,256]{1,2,0:T(8,128)(2,1)} %stack.2), calls=%async_computation | async-start | bytes 12582912 | tf_op jit(solution)/shard_map/all_to_all | solution.py:92
  25.1 4.2 fusion.19
  29.3 82.4 %all-gather.3.cloned.1.call-done = bf16[384,3072]{1,0:T(8,128)(2,1)} async-done(((bf16[384,384]{1,0:T(8,128)(2,1)}), bf16[384,3072]{1,0:T(8,128)(2,1)}) %all-gather.3.cloned.1.call-update) | async-done | bytes 2359312 | tf_op jit(solution)/shard_map/all_gather | solution.py:78
  111.7 2.2 convert_reduce_fusion.1
  113.9 2.4 multiply_reduce_fusion
  116.3 6.8 %add_convert_fusion = bf16[384,3072]{1,0:T(8,128)(2,1)} fusion(f32[384,3072]{1,0:T(8,128)} %fusion.19, bf16[384,3072]{1,0:T(8,128)(2,1)S(1)} %copy-done.2, f32[384]{0:T(512)S(1)} %add_rsqrt_fusion, f32[384]{0:T(512)S(1)} %broadcast_multiply_fusion, f32[3,4,3072]{2,1,0:T(4,128)S(1)} %copy-done.6, s32[384]{0:T(512)S(1)} %dynamic_slice.23), kind=kOutput, calls=%fused_computation.19 | convolution fusion | flops 64882176 | bytes 9492480 | tf_op jit(solution)/shard_map/dot_general | solution.py:16
  123.2 11.6 %fusion.12 = f32[384,3072]{1,0:T(8,128)} fusion(bf16[768,3072]{1,0:T(8,128)(2,1)} %param.21, bf16[384,3072]{1,0:T(8,128)(2,1)} %add_convert_fusion, bf16[3072,768]{1,0:T(8,128)(2,1)} %param.19), kind=kOutput, calls=%fused_computation.32 | convolution fusion | flops 3626532864 | bytes 16515072 | tf_op jit(solution)/shard_map/dot_general | solution.py:126
  134.8 89.9 %all-to-all-done = bf16[32,384,256]{1,2,0:T(8,128)(2,1)} async-done(((bf16[32,384,256]{1,2,0:T(8,128)(2,1)}), bf16[32,384,256]{1,2,0:T(8,128)(2,1)}, u32[]{:S(2)}, u32[]{:S(2)}) %all-to-all-start) | async-done | bytes 6291488 | tf_op jit(solution)/shard_map/all_to_all | solution.py:92
  224.7 8.6 %copy.36 = bf16[32,384,256]{2,1,0:T(8,128)(2,1)} copy(bf16[32,384,256]{1,2,0:T(8,128)(2,1)} %all-to-all-done) | data formatting | bytes 12582912 | tf_op jit(solution)/shard_map/all_to_all | solution.py:92
  233.8 142.3 %while.15 = (s32[]{:T(128)}, f32[384,2,128]{0,2,1:T(8,128)S(1)}, f32[384,2]{0,1:T(2,128)S(1)}, f32[384,2]{0,1:T(2,128)S(1)}, s32[384]{0:T(512)S(1)}, /*index=5*/...) while((s32[]{:T(128)}, f32[384,2,128]{0,2,1:T(8,128)S(1)}, ...), condition=%wide.region_4.5_spmd.clone, body=%wide.region_1.4_spmd.clone.sunk | while | flops 624334848 | bytes 42750984 | solution.py:114
  241.7 3.3 fusion.51
  244.9 3.7 convert_reduce_fusion.3
  259.4 3.3 fusion.51
  262.7 3.7 convert_reduce_fusion.3
  277.2 3.3 fusion.51
  280.5 3.7 convert_reduce_fusion.3
  295.0 3.3 fusion.51
  298.3 3.7 convert_reduce_fusion.3
  312.8 3.3 fusion.51
  316.1 3.7 convert_reduce_fusion.3
  330.6 3.3 fusion.51
  333.9 3.7 convert_reduce_fusion.3
  348.4 3.3 fusion.51
  351.7 3.7 convert_reduce_fusion.3
  366.2 3.3 fusion.51
  369.5 3.7 convert_reduce_fusion.3
  376.2 5.3 %convolution_add_fusion = f32[384,3072]{1,0:T(8,128)} fusion(f32[384,3072]{1,0:T(8,128)} %fusion.12, bf16[384,256]{0,1:T(8,128)(2,1)S(1)} %bitcast.73, bf16[256,3072]{1,0:T(8,128)(2,1)S(1)} %copy-done), kind=kOutput, calls=%fused_computation.21 | convolution fusion | flops 605159424 | bytes 11206656 | tf_op jit(solution)/shard_map/dot_general | solution.py:125
  381.5 5.1 fusion.21
  386.7 2.7 convert_element_type.21
  389.4 125.2 %reduce-scatter.2.cloned.1.call-done = f32[48,3072]{1,0:T(8,128)} async-done(((f32[384,3072]{1,0:T(8,128)}), f32[48,3072]{1,0:T(8,128)}) %reduce-scatter.2.cloned.1.call-update) | async-done | bytes 589840 | tf_op jit(solution)/shard_map/reduce_scatter | solution.py:124
  514.6 2.3 multiply_add_fusion
  (154 shorter events, 86.4 us)
Async XLA Ops:
  6.5 369.6 %copy-start = (bf16[256,3072]{1,0:T(8,128)(2,1)S(1)}, bf16[256,3072]{1,0:T(8,128)(2,1)}, u32[]{:S(2)}) copy-start(bf16[256,3072]{1,0:T(8,128)(2,1)} %param.20) | copy-start | bytes 4718596
  6.5 105.2 %all-gather.3.cloned.1.call-start = ((), (), s32[]{:S(2)}) async-start(), calls=%async_computation.2 | async-start | bytes 2654208 | tf_op jit(solution)/shard_map/all_gather | solution.py:78
  12.0 10.5 %copy-start.4 = (bf16[384,256]{1,0:T(8,128)(2,1)S(1)}, bf16[384,256]{1,0:T(8,128)(2,1)}, u32[]{:S(2)}) copy-start(bf16[384,256]{1,0:T(8,128)(2,1)} %param.15) | copy-start | bytes 589828
  12.0 11.4 %copy-start.5 = (bf16[384,256]{1,0:T(8,128)(2,1)S(1)}, bf16[384,256]{1,0:T(8,128)(2,1)}, u32[]{:S(2)}) copy-start(bf16[384,256]{1,0:T(8,128)(2,1)} %param.13) | copy-start | bytes 589828
  12.0 12.5 %copy-start.7 = (s32[4]{0:T(128)S(1)}, s32[4]{0:T(128)}, u32[]{:S(2)}) copy-start(s32[4]{0:T(128)} %param.17) | copy-start | bytes 52
  12.0 13.1 %copy-start.6 = (f32[3,4,3072]{2,1,0:T(4,128)S(1)}, f32[3,4,3072]{2,1,0:T(4,128)}, u32[]{:S(2)}) copy-start(f32[3,4,3072]{2,1,0:T(4,128)} %param.18) | copy-start | bytes 442372
  12.0 212.7 %all-to-all-start = ((bf16[32,384,256]{1,2,0:T(8,128)(2,1)}), bf16[32,384,256]{1,2,0:T(8,128)(2,1)}, u32[]{:S(2)}, u32[]{:S(2)}) async-start(bf16[32,384,256]{1,2,0:T(8,128)(2,1)} %stack.2), calls=%async_computation | async-start | bytes 12582912 | tf_op jit(solution)/shard_map/all_to_all | solution.py:92
  22.4 210.9 %all-gather.5.cloned.1.call-start = ((), (), s32[]{:S(2)}) async-start(), calls=%async_computation.3 | async-start | bytes 6488064 | tf_op jit(solution)/shard_map/all_gather | solution.py:93
  23.3 491.4 %reduce-scatter.2.cloned.1.call-start = ((), (), s32[]{:S(2)}) async-start(), calls=%async_computation.4 | async-start | bytes 5308416 | tf_op jit(solution)/shard_map/reduce_scatter | solution.py:124
  111.7 4.6 copy-start.2
  244.9 5.0 copy-start.1
  262.7 5.0 copy-start.1
  280.5 5.0 copy-start.1
  298.3 5.0 copy-start.1
  316.1 5.0 copy-start.1
  333.9 5.0 copy-start.1
  351.7 5.0 copy-start.1
  369.5 5.0 copy-start.1
  381.5 5.1 copy-start.3
Sparse Core Ops, SparseCore 0:
  9.8 101.8 all-gather.2
  113.5 104.5 all-gather.4
  381.6 132.9 reduce-scatter.1
